TPU v7x, 256 devices: a whole 4x4x8 slice. The times are simulated.
256 devices in a mesh: tensor: 64 (over z_lo, x, y, core), dp: 4 (over z_hi).
Axes of the slice: x: 4, y: 4, z: 8 (z_hi: 4, z_lo: 2; z = z_hi * 2 + z_lo), core: 2. Of those that a mesh axis runs over, the one named last changes fastest.
Arguments:
- cotangent: bfloat16 [1024, 8192], P('dp', 'tensor'), may hold values from -12 to 12
- down_weight: bfloat16 [28672, 8192], P('tensor', 'dp'), may hold values from -0.0625 to 0.0625
- gate_pre: bfloat16 [1024, 28672], P('dp', 'tensor'), may hold values from -6 to 6
- up_pre: bfloat16 [1024, 28672], P('dp', 'tensor'), may hold values from -6 to 6
Outputs:
- factor: bfloat16 [64, 2, 33, 4, 50176], P('tensor', None, None, 'dp')
All inputs are finite; a program needn't handle non-finite values.
Results may differ from a plain program's by a relative error of at most 0.0057.
Values may be sent and summed in bfloat16 or wider, within the bound.
A program may use at most 128 MiB of HBM per device.

v0:
```python
import jax
import jax.numpy as jnp
from jax import lax
from jax.sharding import PartitionSpec as P


def per_device(cotangent, down_weight, gate_pre, up_pre):
    block_count = lax.axis_size("tensor")
    groups = lax.axis_size("dp")
    own_block = lax.axis_index("tensor")
    group_index = lax.axis_index("dp")
    local_tokens = gate_pre.shape[0]
    block_width = gate_pre.shape[1]
    slice_width = block_width // groups
    all_tokens = local_tokens * groups
    band_width = block_count // 2 + 1
    contract = (((1,), (1,)), ((), ()))
    features = lax.all_gather(cotangent, "tensor", axis=1, tiled=True)
    hidden_cot = lax.dot_general(
        features,
        lax.all_gather(down_weight, "dp", axis=1, tiled=True),
        contract,
        preferred_element_type=jnp.float32,
    )
    gate_value = gate_pre.astype(jnp.float32)
    up_value = up_pre.astype(jnp.float32)
    sigmoid_gate = jax.nn.sigmoid(gate_value)
    grad_gate = (
        hidden_cot * up_value * sigmoid_gate * (1.0 + gate_value * (1.0 - sigmoid_gate))
    ).astype(jnp.bfloat16)
    grad_up = (hidden_cot * gate_value * sigmoid_gate).astype(jnp.bfloat16)
    stacked = jnp.stack([grad_gate, grad_up])
    own_rows = lax.all_gather(stacked, "dp", axis=1, tiled=True)
    own_slice = lax.dynamic_slice_in_dim(own_rows, group_index * slice_width, slice_width, 2)
    inverse_count = 1.0 / all_tokens

    def factor_tile(partner):
        product = jnp.einsum("ftr,ftc->frc", own_rows, partner, preferred_element_type=jnp.float32)
        return (product * inverse_count).astype(jnp.bfloat16)

    def place(result, offset, partner):
        return lax.dynamic_update_slice(
            result,
            factor_tile(partner)[:, None],
            (jnp.int32(0), offset, jnp.int32(0), jnp.int32(0)),
        )

    holder = jnp.zeros((2, band_width, block_width, slice_width), jnp.bfloat16)
    block_piece = lax.all_gather(own_slice[None], "tensor", axis=0, tiled=True)

    def place_block(position, current):
        offset = (own_block - position) % block_count
        partner = lax.dynamic_index_in_dim(block_piece, position, 0, keepdims=False)
        return lax.cond(
            offset < band_width,
            lambda kept: place(kept, offset, partner),
            lambda kept: kept,
            current,
        )

    factor = lax.fori_loop(0, block_piece.shape[0], place_block, holder)
    flat = factor.reshape(2, band_width, block_width * slice_width)
    return flat[None, :, :, None, :]


def solution(mesh):
    placed = (P("dp", "tensor"), P("tensor", "dp"), P("dp", "tensor"), P("dp", "tensor"))
    return jax.shard_map(
        per_device,
        mesh=mesh,
        in_specs=placed,
        out_specs=P("tensor", None, None, "dp", None),
        check_vma=False,
    )
```

profile of v0, /device:TPU:1, one launch (start us, length us, event | category | flops | bytes accessed | tf_op | source)
XLA Modules:
  0.0 617.8 jit_solution(3863569441559747056)
XLA Ops:
  8.1 121.4 %all-gather.6.cloned.1.call-done = bf16[256,8192]{1,0:T(8,128)(2,1)} async-done(((bf16[256,128]{1,0:T(8,128)(2,1)}), bf16[256,8192]{1,0:T(8,128)(2,1)}) %all-gather.6.cloned.1.call-update) | async-done | bytes 4194320 | tf_op jit(solution)/shard_map/all_gather | solution.py:18
  129.5 137.8 %all-gather.8.cloned.1.call-done = bf16[448,8192]{1,0:T(8,128)(2,1)} async-done(((bf16[448,2048]{1,0:T(8,128)(2,1)}), bf16[448,8192]{1,0:T(8,128)(2,1)}) %all-gather.8.cloned.1.call-update) | async-done | bytes 7340048 | tf_op jit(solution)/shard_map/all_gather | solution.py:21
  267.3 6.5 %fusion.15 = (bf16[1,256,448]{1,2,0:T(8,128)(2,1)S(1)}, bf16[1,256,448]{1,2,0:T(8,128)(2,1)S(1)}) fusion(bf16[256,448]{0,1:T(8,128)(2,1)} %param.10, bf16[256,448]{0,1:T(8,128)(2,1)} %param.11, bf16[256,8192]{1,0:T(8,128)(2,1)} %all-gather.6.cloned.1.call-done, bf16[448,8192]{1,0:T(8,128)(2,1)} %all-gather.8.cloned.1.call-done), kind=kOutput, calls=%fused_computation.20 | convolution fusion | flops 1880768512 | bytes 12451840 | tf_op jit(solution)/shard_map/dot_general | solution.py:19
  274.7 50.5 %all-gather.10.cloned.1.call-done = bf16[2,1024,448]{1,2,0:T(8,128)(2,1)} async-done(((bf16[2,256,448]{1,2,0:T(8,128)(2,1)}), bf16[2,1024,448]{1,2,0:T(8,128)(2,1)}) %all-gather.10.cloned.1.call-update) | async-done | bytes 1835024 | tf_op jit(solution)/shard_map/all_gather | solution.py:33
  327.2 167.3 %all-gather.12.cloned.1.call-done = bf16[128,1024,112]{1,2,0:T(8,128)(2,1)} async-done(((bf16[2,1024,112]{1,2,0:T(8,128)(2,1)}), bf16[128,1024,112]{1,2,0:T(8,128)(2,1)}) %all-gather.12.cloned.1.call-update) | async-done | bytes 29360144 | tf_op jit(solution)/shard_map/all_gather | solution.py:49
  494.4 3.9 broadcast_in_dim.10
  498.4 80.2 %while.18 = (s32[]{:T(128)}, bf16[2,33,448,112]{2,3,0,1:T(8,128)(2,1)}, s32[]{:T(128)}, bf16[64,2,1024,112]{2,3,1,0:T(8,128)(2,1)}, bf16[2,1024,448]{1,2,0:T(8,1...) while((s32[]{:T(128)}, bf16[2,33,448,112]{2,3,0,1:T(8,128)(2,1)}, s32[]{:T(128)}, ...), condition=%wide.region_3.4_spmd, body=%wide.region_0.3_spmd.sunk | while | flops 205721616 | bytes 2523496 | solution.py:61
  498.4 2.4 conditional.2
  498.4 2.4 fusion.2
  500.8 2.4 conditional.2
  500.8 2.4 fusion.2
  504.5 2.4 conditional.2
  504.6 2.4 fusion.2
  509.4 2.4 conditional.2
  509.4 2.4 fusion.2
  511.7 2.4 conditional.2
  511.7 2.4 fusion.2
  514.1 2.4 conditional.2
  514.1 2.4 fusion.2
  516.5 2.4 conditional.2
  516.5 2.4 fusion.2
  518.9 2.4 conditional.2
  518.9 2.4 fusion.2
  521.3 2.4 conditional.2
  521.3 2.4 fusion.2
  526.1 2.4 conditional.2
  526.1 2.4 fusion.2
  528.5 2.4 conditional.2
  528.5 2.4 fusion.2
  530.9 2.4 conditional.2
  530.9 2.4 fusion.2
  533.2 2.4 conditional.2
  533.2 2.4 fusion.2
  535.6 2.4 conditional.2
  538.0 2.4 conditional.2
  540.4 2.4 conditional.2
  540.4 2.4 fusion.2
  542.8 2.4 conditional.2
  542.8 2.4 fusion.2
  545.2 2.4 conditional.2
  545.2 2.4 fusion.2
  549.9 2.4 conditional.2
  552.3 2.4 conditional.2
  552.3 2.4 fusion.2
  554.7 2.4 conditional.2
  554.7 2.4 fusion.2
  557.1 2.4 conditional.2
  557.1 2.4 fusion.2
  559.5 2.4 conditional.2
  559.5 2.4 fusion.2
  561.9 2.4 conditional.2
  561.9 2.4 fusion.2
  564.3 2.4 conditional.2
  564.3 2.4 fusion.2
  566.7 2.4 conditional.2
  566.7 2.4 fusion.2
  569.1 2.4 conditional.2
  569.1 2.4 fusion.2
  573.8 2.4 conditional.2
  573.8 2.4 fusion.2
  576.2 2.4 conditional.2
  576.2 2.4 fusion.2
  578.6 10.8 %copy.6 = bf16[2,33,448,112]{3,2,0,1:T(8,128)(2,1)} copy(bf16[2,33,448,112]{2,3,0,1:T(8,128)(2,1)} %get-tuple-element.191) | data formatting | bytes 13246464 | tf_op jit(solution)/shard_map/while | solution.py:61
  589.5 21.8 %broadcast_in_dim_reshape.3 = bf16[1,2,33,1,50176]{4,1,3,2,0:T(2,128)(2,1)} reshape(bf16[2,33,448,112]{3,2,0,1:T(8,128)(2,1)} %copy.6) | data formatting | bytes 13246464 | tf_op jit(solution)/shard_map/broadcast_in_dim;reshape | solution.py:63
  (54 shorter events, 30.7 us)
Async XLA Ops:
  6.5 122.9 %all-gather.6.cloned.1.call-start = ((), (), s32[]{:S(2)}) async-start(), calls=%async_computation | async-start | bytes 4259840 | tf_op jit(solution)/shard_map/all_gather | solution.py:18
  7.3 260.0 %all-gather.8.cloned.1.call-start = ((), (), s32[]{:S(2)}) async-start(), calls=%async_computation.1 | async-start | bytes 9175040 | tf_op jit(solution)/shard_map/all_gather | solution.py:21
  8.0 317.2 %all-gather.10.cloned.1.call-start = ((), (), s32[]{:S(2)}) async-start(), calls=%async_computation.2 | async-start | bytes 2293760 | tf_op jit(solution)/shard_map/all_gather | solution.py:33
  274.7 219.8 %all-gather.12.cloned.1.call-start = ((), (), s32[]{:S(2)}) async-start(), calls=%async_computation.3 | async-start | bytes 29818880 | tf_op jit(solution)/shard_map/all_gather | solution.py:49
  325.2 173.2 %copy-start = (bf16[2,1024,448]{1,2,0:T(8,128)(2,1)S(1)}, bf16[2,1024,448]{1,2,0:T(8,128)(2,1)}, u32[]{:S(2)}) copy-start(bf16[2,1024,448]{1,2,0:T(8,128)(2,1)} %all-gather.10.cloned.1.call-done) | copy-start | bytes 5505028
Sparse Core Ops, SparseCore 0:
  9.1 120.3 all-gather.5
  131.3 135.9 all-gather.7
  274.8 50.3 all-gather.9
  327.3 167.1 all-gather.11
where the time goes:
time: 620 us; the launch traced here: 618 us
  waiting for transfers between devices  478 us (77%)
  matrix products  85.4 us (14%)
  local copies, waits for them, and re-layouts  38.5 us (6%)
  between operations  13.1 us (2%)
    all_gather x1, waiting for transfers between devices, per_device(): block_piece = lax.all_gather(own_slice[None], 'tensor', axis=0, tiled=True)  167 us
    all_gather x1, waiting for transfers between devices, per_device(): lax.all_gather(down_weight, 'dp', axis=1, tiled=True)  138 us
    all_gather x1, waiting for transfers between devices, per_device(): features = lax.all_gather(cotangent, 'tensor', axis=1, tiled=True)  121 us
    dot_general x33, matrix products, factor_tile(): jnp.einsum('ftr,ftc->frc', own_rows, partner, preferred_element_type=jnp....  78.8 us
    all_gather x1, waiting for transfers between devices, per_device(): own_rows = lax.all_gather(stacked, 'dp', axis=1, tiled=True)  50.5 us
    another operation x1, local copies, waits for them, and re-layouts, per_device(): return flat[None, :, :, None, :]  21.8 us
  transfers between devices with their start and end apart: 4, of which 4 were waited for; matrix products, arithmetic and copies ran while one was open for 0% of the time, Pallas kernels for 0%

commit v1 on v0

v1 whole, which is shorter than its diff:
```python
import jax
import jax.numpy as jnp
from jax import lax
from jax.experimental import pallas as pl
from jax.experimental.pallas import tpu as pltpu
from jax.sharding import PartitionSpec as P

MESH = pl.DeviceIdType.MESH
NT = (((1,), (1,)), ((), ()))
F32 = jnp.float32
BF16 = jnp.bfloat16


def kernel(c_ref, w_ref, gate_ref, up_ref, y_ref,
           cq, hp, hf, hr, gu, rows, grouped, blocks, stage,
           s_send, s_cin, s_c, s_gu, s_h, s_rows, s_blk, s_loc):
    t = lax.axis_index("tensor")
    g = lax.axis_index("dp")
    core = t % 2
    y = (t // 2) % 4
    x = (t // 8) % 4
    zl = t // 32
    lt = c_ref.shape[0]
    sw = hp.shape[2]
    tokens = 4 * lt
    inv = 1.0 / tokens

    def tid(zz, xx, yy, cc):
        return ((zz * 4 + xx) * 4 + yy) * 2 + cc

    xp, xm = (x + 1) % 4, (x + 3) % 4
    yp, ym, y2 = (y + 1) % 4, (y + 3) % 4, (y + 2) % 4
    d_xp, d_xm = (tid(zl, xp, y, core), g), (tid(zl, xm, y, core), g)
    d_yp, d_ym = (tid(zl, x, yp, core), g), (tid(zl, x, ym, core), g)
    d_sib = (tid(zl, x, y, 1 - core), g)
    d_z = (tid(1 - zl, x, y, core), g)
    gp, gm, g2 = (g + 1) % 4, (g + 3) % 4, (g + 2) % 4
    d_gp, d_gm, d_g2 = (t, gp), (t, gm), (t, g2)
    d_zg = [(tid(1 - zl, x, y, core), q) for q in (gp, gm, g2)]

    barrier = pltpu.get_barrier_semaphore()
    friends = [d_xp, d_xm, d_yp, d_ym, d_sib, d_z, d_gp, d_gm, d_g2] + d_zg
    for d in friends:
        pl.semaphore_signal(barrier, inc=1, device_id=d, device_id_type=MESH)
    pl.semaphore_wait(barrier, len(friends))

    pending = []

    def send(src, dst, sem, dev, cond=None):
        copy = pltpu.make_async_remote_copy(
            src_ref=src, dst_ref=dst, send_sem=s_send.at[len(pending)], recv_sem=sem,
            device_id=dev, device_id_type=MESH)
        if cond is None:
            copy.start()
        else:
            pl.when(cond)(copy.start)
        pending.append((cond, copy))

    def arrived(ref, sem, cond=None):
        wait = pltpu.make_async_copy(ref, ref, sem).wait
        if cond is None:
            wait()
        else:
            pl.when(cond)(wait)

    home = t // 16
    slot = t % 16
    for p in range(2):
        me = (zl == p) & (home == g)
        dst = cq.at[g, slot]
        send(c_ref, dst, s_cin.at[g], (p * 32 + t % 32, home), jnp.logical_not(me))

        @pl.when(me)
        def _():
            own = pltpu.make_async_copy(c_ref, dst, s_loc)
            own.start()
            own.wait()

    def send_gate_up():
        for q, d in ((g2, d_g2), (gp, d_gp), (gm, d_gm)):
            for i, ref in enumerate((gate_ref, up_ref)):
                send(ref.at[pl.ds(q * sw, sw)], gu.at[i, g], s_gu.at[i, g], d)

    rel = (x + 4 - 2 * (g % 2)) % 4
    owner = rel < 2
    first = jnp.where((rel == 0) | (rel == 3), 0, 1)
    second = 1 - first

    def cslot(col, yy):
        return col * 8 + yy * 2 + core

    def c_send(q, j, dev, cond=None):
        send(cq.at[q, j], cq.at[q, j], s_c.at[q, j], dev, cond)

    def c_got(q, j, cond=None):
        arrived(cq.at[q, j], s_c.at[q, j], cond)

    def c_spread(q, j):
        c_send(q, j, d_yp)
        c_send(q, j, d_ym)
        c_send(q, j, d_sib)

    j1, j2 = cslot(first, y), cslot(second, y)

    def c0(q):
        mine = (zl == g // 2) & (g == q)
        arrived(cq.at[q, slot], s_cin.at[q], owner & jnp.logical_not(mine))
        c_got(q, j1, jnp.logical_not(owner))
        c_send(q, j1, d_xp, rel != 3)
        c_send(q, j1, d_xm, rel != 2)
        c_spread(q, j1)

    def c1(q):
        c_got(q, j2)
        c_spread(q, j2)

    def c_hop(q, col):
        j = cslot(col, ym)
        c_got(q, j)
        c_send(q, j, d_yp, col == 0)
        c_send(q, j, d_sib)
        j = cslot(col, yp)
        c_got(q, j)
        c_send(q, j, d_ym, col == 1)
        c_send(q, j, d_sib)

    def c2(q):
        c_hop(q, first)

    def c3(q):
        c_hop(q, second)

    def c4(q):
        for col in range(2):
            j = cslot(col, y2)
            c_got(q, j)
            c_send(q, j, d_sib)

    def partial(q):
        for i in range(8):
            c_got(q, i * 2 + 1 - core)
        right = jnp.concatenate([cq[q, j] for j in range(16)], axis=1)
        product = lax.dot_general(w_ref[...], right, NT, preferred_element_type=F32)
        for s in range(4):
            part = product[s * sw:(s + 1) * sw]
            hf[q, s] = part
            hp[s, q] = part.astype(BF16)
        for s, d in ((g2, d_g2), (gp, d_gp), (gm, d_gm)):
            send(hp.at[s, q], hr.at[g, q], s_h.at[g, q], d)

    def gradients(q):
        if q == 0:
            for s in (gp, gm, g2):
                for i in range(2):
                    arrived(gu.at[i, s], s_gu.at[i, s])
            own = pl.ds(pl.multiple_of(g * sw, 16), sw)
            gu[0, g] = gate_ref[own, :]
            gu[1, g] = up_ref[own, :]
        for s in (gp, gm, g2):
            arrived(hr.at[s, q], s_h.at[s, q])
        total = hf[q, g]
        for s in (gp, gm, g2):
            total = total + hr[s, q].astype(F32)
        gate = gu[0, q].astype(F32)
        up = gu[1, q].astype(F32)
        sig = jax.nn.sigmoid(gate)
        grads = (total * up * sig * (1.0 + gate * (1.0 - sig)), total * gate * sig)
        for f in range(2):
            value = grads[f].astype(BF16)
            rows[q, g, f] = value
            blocks[f, q, 0, 0:sw] = value

    def unit(q, m):
        return blocks.at[:, q, m, 0:sw]

    def pass_on(q, m_from, dev, m_to, cond=None):
        send(unit(q, m_from), unit(q, m_to), s_blk.at[q, m_to], dev, cond)

    def got(q, m, cond=None):
        arrived(unit(q, m), s_blk.at[q, m], cond)

    def to_sibling(q, m, cond=None):
        pass_on(q, m, d_sib, 17 if isinstance(m, int) and m == 16 else 18 + m, cond)

    def ahead(q, p):
        return (p != 2) if q % 2 == 0 else (p == 1)

    def behind(q, p):
        return (p == 2) if q % 2 == 0 else (p != 1)

    dyp, dym = yp - y, ym - y

    def rows_out(q):
        for d in (d_gp, d_gm):
            send(rows.at[q, g], rows.at[q, g], s_rows.at[q, g], d)

    def rows_on(q):
        for s, other, d in ((gm, 0, d_gp), (gp, 1, d_gm)):
            arrived(rows.at[q, s], s_rows.at[q, s])
            if q % 2 == other:
                send(rows.at[q, s], rows.at[q, s], s_rows.at[q, s], d)

    def b0(q):
        pass_on(q, 0, d_z, 16)
        pass_on(q, 0, d_xp, 4, x < 3)
        pass_on(q, 0, d_xm, 12, x == 0)
        pass_on(q, 0, d_yp, (dyp + 16) % 16, y < 3)
        pass_on(q, 0, d_ym, (dym + 16) % 16, y == 0)
        to_sibling(q, 0, core == 0)

    def b1(q):
        got(q, 16)
        pass_on(q, 16, d_xp, 4, x == 3)
        pass_on(q, 16, d_xm, 12, x > 0)
        pass_on(q, 16, d_yp, (dyp + 16) % 16, y == 3)
        pass_on(q, 16, d_ym, (dym + 16) % 16, y > 0)
        to_sibling(q, 16, core == 1)

    def spread_y(q, m):
        pass_on(q, m, d_yp, (m + dyp + 16) % 16)
        pass_on(q, m, d_ym, (m + dym + 16) % 16)
        to_sibling(q, m)

    def b2(q):
        got(q, 4)
        pass_on(q, 4, d_xp, 8, ahead(q, xm))
        spread_y(q, 4)
        got(q, 12)
        pass_on(q, 12, d_xm, 8, behind(q, xp))
        spread_y(q, 12)

    def b3(q):
        got(q, 8)
        spread_y(q, 8)

    def b4(base):
        def run(q):
            m = (base + y - ym + 16) % 16
            got(q, m)
            if base == 0:
                pass_on(q, m, d_yp, (m + dyp + 16) % 16, ahead(q, ym))
            elif q % 2 == 0:
                pass_on(q, m, d_yp, (m + dyp + 16) % 16)
            to_sibling(q, m)
            m = (base + y - yp + 16) % 16
            got(q, m)
            if base == 0:
                pass_on(q, m, d_ym, (m + dym + 16) % 16, behind(q, yp))
            elif q % 2 == 1:
                pass_on(q, m, d_ym, (m + dym + 16) % 16)
            to_sibling(q, m)
        return run

    def spare(d):
        return 33 + (d + 4) % 4

    def slot_o(d):
        return jnp.where(d > 0, d, spare(d))

    def slot_x(d):
        return jnp.where(d < 0, 16 + d, spare(d))

    def along_x(q, d):
        so, sx = slot_o(d), slot_x(d)
        pass_on(q, jnp.where(x < 3, so, sx), d_xp, (20 + d) % 16)
        pass_on(q, jnp.where(x == 0, so, sx), d_xm, (28 + d) % 16)

    def y0(q):
        pass_on(q, 0, d_z, 16)
        pass_on(q, 0, d_yp, slot_o(dyp))
        pass_on(q, 0, d_ym, slot_o(dym))
        pass_on(q, 0, d_xp, 4, x < 3)
        pass_on(q, 0, d_xm, 12, x == 0)
        to_sibling(q, 0, core == 0)

    def y1(q):
        got(q, 16)
        pass_on(q, 16, d_yp, slot_x(dyp))
        pass_on(q, 16, d_ym, slot_x(dym))
        pass_on(q, 16, d_xp, 4, x == 3)
        pass_on(q, 16, d_xm, 12, x > 0)
        to_sibling(q, 16, core == 1)

    def y_hop(q, source, dest, dev, forward):
        d = y - source
        for pick in (slot_o, slot_x):
            got(q, pick(d))
            if forward:
                pass_on(q, pick(d), dev, pick(dest - source))
        along_x(q, d)
        to_sibling(q, (d + 16) % 16)

    def y2a(q):
        y_hop(q, ym, yp, d_yp, q % 2 == 0)
        y_hop(q, yp, ym, d_ym, q % 2 == 1)

    def y3(q):
        y_hop(q, y2, None, None, False)

    def y4(source):
        def run(q):
            d = y - source
            m = (20 + d) % 16
            got(q, m)
            pass_on(q, m, d_xp, (24 + d) % 16, ahead(q, xm))
            to_sibling(q, m)
            m = (28 + d) % 16
            got(q, m)
            pass_on(q, m, d_xm, (24 + d) % 16, behind(q, xp))
            to_sibling(q, m)
        return run

    def y4b(q):
        y4(ym)(q)
        y4(yp)(q)

    def y5(q, source):
        m = (24 + y - source) % 16
        got(q, m)
        to_sibling(q, m)

    def start(q):
        gradients(q)
        (b0 if q < 2 else y0)(q)

    lead = [c0, c1, c2, c3, c4, partial]
    for wave in range(8):
        for q in range(4):
            if 0 <= wave - q < len(lead):
                lead[wave - q](q)
        if wave == 0:
            send_gate_up()
    start(0)
    partial(3)
    start(1)
    b1(0)
    start(2)
    b1(1)
    start(3)
    y1(2)
    y1(3)
    for q in range(4):
        rows_out(q)
    b2(0)
    y2a(2)
    b2(1)
    y2a(3)
    b3(0)
    b3(1)
    y3(2)
    y3(3)
    for q in range(4):
        (b4(0) if q < 2 else y4(y))(q)
    for q in range(4):
        rows_on(q)
    for base, late_y in ((4, y4b), (12, y4(y2)), (8, None)):
        for q in (0, 1):
            b4(base)(q)
        if late_y is not None:
            for q in (2, 3):
                late_y(q)
    for q in (2, 3):
        for source in (y, ym, yp):
            y5(q, source)
    for q in range(4):
        arrived(rows.at[q, g2], s_rows.at[q, g2])

    per_class = sw // 8
    target = lax.broadcasted_iota(jnp.int32, (128, sw), 0)
    source = lax.broadcasted_iota(jnp.int32, (128, sw), 1)
    pick = ((target % 16 < per_class) & (source == 8 * (target % 16) + target // 16)).astype(BF16)
    for f in range(2):
        for q in range(4):
            for s in range(4):
                moved = jnp.dot(pick, rows[q, s, f], preferred_element_type=F32)
                grouped[f, s, :, q * lt:(q + 1) * lt] = moved.astype(BF16)
    lane = lax.broadcasted_iota(jnp.int32, (16, 128), 1)

    def pair_of(i):
        late = jnp.where(i < 13, 2 * i - 17, 2 * i - 16)
        return jnp.where(i < 4, 2 * i, jnp.where(i < 5, 8, jnp.where(i < 9, 2 * i - 1, late)))

    def wanted(at):
        return jnp.where(core == 0, at != 18, at != 17)

    def place(at, half):
        k = jnp.where(at < 17, 2 * at, jnp.where(at == 17, 31, 2 * (at - 18) + 2 * core - 1))

        @pl.when(wanted(at))
        def _():
            y_ref[jnp.maximum(k, 0)] = stage[half, 0:y_ref.shape[1], :].astype(BF16)

    def step(i):
        p = pair_of(i)
        for f in range(2):
            left = grouped[f].reshape(512, tokens)
            right = jnp.concatenate(
                [blocks[f, q, pl.ds(2 * p, 2)].reshape(256, lt) for q in range(4)], axis=1)
            product = lax.dot_general(left, right, NT, preferred_element_type=F32)
            for half in range(2):
                tile = product[:, half * 128:half * 128 + 128] * inv
                for s in range(4):
                    turned = [
                        pltpu.roll(tile[s * 128 + r * 16:s * 128 + r * 16 + 16], (128 - 16 * r) % 128, 1)
                        for r in range(8)
                    ]
                    for r in range(7):
                        merged = jnp.where(lane < 112 - 16 * r, turned[r], turned[r + 1])
                        stage[half, pl.ds(14 * per_class * s + 2 * r + f, 16, stride=14), :] = merged
        for half in range(2):
            place(2 * p + half, half)

    base_index = len(pending)
    assert base_index + 8 <= s_send.shape[0], base_index

    def far(i, q):
        m = 4 * i + 2
        return pltpu.make_async_remote_copy(
            src_ref=unit(q, m), dst_ref=unit(q, 18 + m), send_sem=s_send.at[base_index + 2 * i + q],
            recv_sem=s_blk.at[q, 18 + m], device_id=d_sib, device_id_type=MESH)

    def from_sibling(m):
        for q in range(4):
            got(q, 18 + m)

    def early(i, _):
        @pl.when(i == 4)
        def _():
            for q in range(4):
                got(q, 17, core == 0)

        @pl.when((i > 5) | ((i == 5) & (core == 1)))
        def _():
            from_sibling(4 * (i - 5))

        @pl.when(i > 4)
        def _():
            from_sibling(4 * (i - 5) + 1)

        step(i)

        @pl.when(i < 4)
        def _():
            for q in range(2):
                got(q, 4 * i + 2)
                far(i, q).start()
        return 0

    def late(i, _):
        @pl.when(i > 12)
        def _():
            from_sibling(4 * (i - 13) + 2)
            from_sibling(4 * (i - 13) + 3)

        step(i)
        return 0

    lax.fori_loop(0, 9, early, 0)
    for q in (2, 3):
        y5(q, y2)
    lax.fori_loop(9, 17, late, 0)
    for i in range(4):
        for q in range(2):
            far(i, q).wait_send()
    for cond, copy in pending:
        if cond is None:
            copy.wait_send()
        else:
            pl.when(cond)(copy.wait_send)


def per_device(cotangent, down_weight, gate_pre, up_pre):
    groups = lax.axis_size("dp")
    lt, bw = gate_pre.shape
    sw = bw // groups
    tokens = lt * groups
    tile_rows = bw * sw // 128
    vm, dma = pltpu.VMEM, pltpu.SemaphoreType.DMA
    out = pl.pallas_call(
        kernel,
        out_shape=vm((33, 2 * tile_rows, 128), BF16),
        in_specs=[pl.BlockSpec(memory_space=pltpu.VMEM)] * 4,
        out_specs=pl.BlockSpec(memory_space=pltpu.VMEM),
        scratch_shapes=[
            vm((4, 16, lt, 128), BF16),
            vm((4, 4, sw, lt), BF16),
            vm((4, 4, sw, lt), F32),
            vm((4, 4, sw, lt), BF16),
            vm((2, 4, sw, lt), BF16),
            vm((4, 4, 2, sw, lt), BF16),
            vm((2, 4, 128, tokens), BF16),
            vm((2, 4, 37, 128, lt), BF16),
            vm((2, 2 * tile_rows + 32, 128), F32),
            dma((320,)), dma((4,)), dma((4, 16)), dma((2, 4)), dma((4, 4)), dma((4, 4)), dma((4, 37)),
            dma(()),
        ],
        compiler_params=pltpu.CompilerParams(collective_id=0, has_side_effects=True, vmem_limit_bytes=50 << 20),
    )(cotangent, down_weight, gate_pre.T, up_pre.T)
    out = out.reshape(33, tile_rows, 2, 128)
    out = jnp.transpose(out, (2, 0, 1, 3)).reshape(2, 33, bw * sw)
    return out[None, :, :, None, :]


def solution(mesh):
    placed = (P("dp", "tensor"), P("tensor", "dp"), P("dp", "tensor"), P("dp", "tensor"))
    return jax.shard_map(
        per_device,
        mesh=mesh,
        in_specs=placed,
        out_specs=P("tensor", None, None, "dp", None),
        check_vma=False,
    )
```

time: 620 us -> 133 us (0.21)
  waiting for transfers between devices: 478 us -> 0 us
  Pallas kernels: 0 us -> 128 us
  matrix products: 85.4 us -> 0 us
  local copies, waits for them, and re-layouts: 38.5 us -> 2.81 us
  between operations: 13.1 us -> 0.01 us
    all_gather x4 -> x0, waiting for transfers between devices: 477 us -> none  [the longest x1 167 us: per_device(): block_piece = lax.all_gather(own_slice[None], 'tensor', axis=0, tiled=True)]
    pallas_call x0 -> x1, Pallas kernels: none -> 128 us  [per_device(): pl.pallas_call(kernel, out_shape=vm((33, 2 * tile_rows, 128), BF16), in_s...]
    dot_general x34 -> x0, matrix products: 85.4 us -> none  [the longest x33 78.8 us: factor_tile(): jnp.einsum('ftr,ftc->frc', own_rows, partner, preferred_element_type=jnp....]
    another operation x1 -> x0, local copies, waits for them, and re-layouts: 21.8 us -> none  [per_device(): return flat[None, :, :, None, :]]
    while x1 -> x0, local copies, waits for them, and re-layouts: 10.8 us -> none  [per_device(): factor = lax.fori_loop(0, block_piece.shape[0], place_block, holder)]
  transfers between devices with their start and end apart: 4 -> 0, of which waited for: 4 -> 0; matrix products, arithmetic and copies ran while one was open for 0% -> 0% of each run, Pallas kernels for 0% -> 0%
where the time goes in v1:
time: 133 us; the launch traced here: 131 us
  Pallas kernels  128 us (96%)
  local copies, waits for them, and re-layouts  2.81 us (2%)
    pallas_call x1, Pallas kernels, per_device(): pl.pallas_call(kernel, out_shape=vm((33, 2 * tile_rows, 128), BF16), in_s...  128 us
    unnamed x1, local copies, waits for them, and re-layouts  2.81 us

profile of v1, /device:TPU:1, one launch (start us, length us, event | category | flops | bytes accessed | tf_op | source)
XLA Modules:
  0.0 130.5 jit_solution(17780674925687836353)
XLA Ops:
  0.0 127.7 %shard_map.46 = bf16[33,784,128]{2,1,0:T(8,128)(2,1)S(1)} custom-call(bf16[256,128]{1,0:T(8,128)(2,1)} %c_ref.1, bf16[448,2048]{1,0:T(8,128)(2,1)} %w_ref.1, bf16[448,256]{1,0:T(8,128)(2,1)} %bitcast.8, bf16[448,256]{1,0:T(8,128)(2,1)} %bitcast.9), custom_call_target="tpu_custom_call" | custom-call | tf_op jit(solution)/shard_map/pallas_call | solution.py:479
  127.7 2.8 %copy.7 = bf16[1,2,33,1,50176]{4,1,3,2,0:T(2,128)(2,1)} copy(bf16[1,2,33,1,50176]{4,1,3,2,0:T(2,128)(2,1)S(1)} %bitcast.7) | data formatting | bytes 13246464

commit v2 on v1

--- a/solution.py
+++ b/solution.py
@@ -12,7 +12,7 @@
 
 
 def kernel(c_ref, w_ref, gate_ref, up_ref, y_ref,
-           cq, hp, hf, hr, gu, rows, grouped, blocks, stage,
+           cq, hp, hf, hr, gu, rows, grouped, blocks, held, stage,
            s_send, s_cin, s_c, s_gu, s_h, s_rows, s_blk, s_loc):
     t = lax.axis_index("tensor")
     g = lax.axis_index("dp")
@@ -221,12 +221,14 @@
         pass_on(q, m, d_ym, (m + dym + 16) % 16)
         to_sibling(q, m)
 
-    def b2(q):
+    def b2x(q):
         got(q, 4)
         pass_on(q, 4, d_xp, 8, ahead(q, xm))
-        spread_y(q, 4)
         got(q, 12)
         pass_on(q, 12, d_xm, 8, behind(q, xp))
+
+    def b2y(q):
+        spread_y(q, 4)
         spread_y(q, 12)
 
     def b3(q):
@@ -281,21 +283,29 @@
         pass_on(q, 16, d_xm, 12, x > 0)
         to_sibling(q, 16, core == 1)
 
-    def y_hop(q, source, dest, dev, forward):
+    def y_got(q, source, dest, dev, forward):
         d = y - source
         for pick in (slot_o, slot_x):
             got(q, pick(d))
             if forward:
                 pass_on(q, pick(d), dev, pick(dest - source))
+
+    def y_use(q, source):
+        d = y - source
         along_x(q, d)
         to_sibling(q, (d + 16) % 16)
 
-    def y2a(q):
-        y_hop(q, ym, yp, d_yp, q % 2 == 0)
-        y_hop(q, yp, ym, d_ym, q % 2 == 1)
+    def y2f(q):
+        y_got(q, ym, yp, d_yp, q % 2 == 0)
+        y_got(q, yp, ym, d_ym, q % 2 == 1)
+
+    def y2x(q):
+        y_use(q, ym)
+        y_use(q, yp)
 
     def y3(q):
-        y_hop(q, y2, None, None, False)
+        y_got(q, y2, None, None, False)
+        y_use(q, y2)
 
     def y4(source):
         def run(q):
@@ -314,56 +324,62 @@
         y4(ym)(q)
         y4(yp)(q)
 
-    def y5(q, source):
-        m = (24 + y - source) % 16
-        got(q, m)
-        to_sibling(q, m)
+    def rows_end(q):
+        arrived(rows.at[q, g2], s_rows.at[q, g2])
 
     def start(q):
         gradients(q)
         (b0 if q < 2 else y0)(q)
 
     lead = [c0, c1, c2, c3, c4, partial]
-    for wave in range(8):
+    for wave in range(12):
         for q in range(4):
-            if 0 <= wave - q < len(lead):
-                lead[wave - q](q)
+            if 0 <= wave - 2 * q < len(lead):
+                lead[wave - 2 * q](q)
         if wave == 0:
             send_gate_up()
     start(0)
-    partial(3)
     start(1)
+    start(2)
+    start(3)
     b1(0)
-    start(2)
     b1(1)
-    start(3)
+    b2x(0)
     y1(2)
+    b2x(1)
     y1(3)
     for q in range(4):
         rows_out(q)
-    b2(0)
-    y2a(2)
-    b2(1)
-    y2a(3)
+    y2f(2)
+    b2y(0)
+    y2f(3)
+    b2y(1)
+    y2x(2)
     b3(0)
+    y2x(3)
     b3(1)
+    y4(y)(2)
+    y4(y)(3)
+    b4(0)(0)
+    b4(0)(1)
     y3(2)
     y3(3)
+    rows_on(0)
+    y4b(2)
+    b4(4)(0)
+    y4b(3)
+    b4(4)(1)
+    rows_on(1)
+    b4(12)(0)
+    y4(y2)(2)
+    b4(12)(1)
+    rows_on(2)
+    y4(y2)(3)
+    b4(8)(0)
+    b4(8)(1)
+    rows_on(3)
     for q in range(4):
-        (b4(0) if q < 2 else y4(y))(q)
-    for q in range(4):
-        rows_on(q)
-    for base, late_y in ((4, y4b), (12, y4(y2)), (8, None)):
-        for q in (0, 1):
-            b4(base)(q)
-        if late_y is not None:
-            for q in (2, 3):
-                late_y(q)
-    for q in (2, 3):
-        for source in (y, ym, yp):
-            y5(q, source)
-    for q in range(4):
-        arrived(rows.at[q, g2], s_rows.at[q, g2])
+        rows_end(q)
 
     per_class = sw // 8
     target = lax.broadcasted_iota(jnp.int32, (128, sw), 0)
@@ -376,92 +392,100 @@
                 grouped[f, s, :, q * lt:(q + 1) * lt] = moved.astype(BF16)
     lane = lax.broadcasted_iota(jnp.int32, (16, 128), 1)
 
+    order = (0, 8, 9, 6, 15, 1, 7, 10, 16, 2, 4, 11, 13, 3, 5, 12, 14)
+
     def pair_of(i):
-        late = jnp.where(i < 13, 2 * i - 17, 2 * i - 16)
-        return jnp.where(i < 4, 2 * i, jnp.where(i < 5, 8, jnp.where(i < 9, 2 * i - 1, late)))
-
-    def wanted(at):
-        return jnp.where(core == 0, at != 18, at != 17)
-
-    def place(at, half):
-        k = jnp.where(at < 17, 2 * at, jnp.where(at == 17, 31, 2 * (at - 18) + 2 * core - 1))
-
-        @pl.when(wanted(at))
-        def _():
-            y_ref[jnp.maximum(k, 0)] = stage[half, 0:y_ref.shape[1], :].astype(BF16)
+        p = jnp.int32(0)
+        for at, value in enumerate(order):
+            p = jnp.where(i == at, value, p)
+        return p
+
+    def product(p, f):
+        left = grouped[f].reshape(512, tokens)
+        right = jnp.concatenate(
+            [blocks[f, q, pl.ds(2 * p, 2)].reshape(256, lt) for q in range(4)], axis=1)
+        held[f] = lax.dot_general(left, right, NT, preferred_element_type=F32)
+
+    def regroup(f):
+        for half in range(2):
+            for s in range(4):
+                turned = [
+                    pltpu.roll(
+                        held[f, s * 128 + r * 16:s * 128 + r * 16 + 16, half * 128:half * 128 + 128] * inv,
+                        (128 - 16 * r) % 128, 1)
+                    for r in range(8)
+                ]
+                for r in range(7):
+                    merged = jnp.where(lane < 112 - 16 * r, turned[r], turned[r + 1])
+                    stage[half, pl.ds(14 * per_class * s + 2 * r + f, 16, stride=14), :] = merged
+
+    def put_tiles(p):
+        for half in range(2):
+            at = 2 * p + half
+            k = jnp.where(at < 17, 2 * at, jnp.where(at == 17, 31, 2 * (at - 18) + 2 * core - 1))
+            k = jnp.where(k < 0, 1, k)
+            y_ref[k] = stage[half, 0:y_ref.shape[1], :].astype(BF16)
 
     def step(i):
+        for f in range(2):
+            regroup(f)
+            product(pair_of(i), f)
+        put_tiles(pair_of(i - 1))
+
+    base_index = len(pending)
+    assert base_index + 16 <= s_send.shape[0], base_index
+
+    def last_hop(n, q, m):
+        got(q, m)
+        pltpu.make_async_remote_copy(
+            src_ref=unit(q, m), dst_ref=unit(q, 18 + m), send_sem=s_send.at[base_index + n],
+            recv_sem=s_blk.at[q, 18 + m], device_id=d_sib, device_id_type=MESH).start()
+
+    def x_far(source, q):
+        at = {id(y): 0, id(ym): 1, id(yp): 2, id(y2): 3}[id(source)]
+        last_hop(at * 2 + q - 2, q, (24 + y - source) % 16)
+
+    def y_far():
+        for b in range(4):
+            for q in range(2):
+                last_hop(8 + b * 2 + q, q, 4 * b + 2)
+
+    after = {
+        1: [lambda: x_far(y, 2), lambda: x_far(y, 3)], 2: [lambda: x_far(ym, 2)], 3: [lambda: x_far(ym, 3)],
+        4: [y_far], 6: [lambda: x_far(yp, 2)], 8: [lambda: x_far(yp, 3)],
+        10: [lambda: x_far(y2, 2)], 12: [lambda: x_far(y2, 3)],
+    }
+
+    def body(i, _):
         p = pair_of(i)
-        for f in range(2):
-            left = grouped[f].reshape(512, tokens)
-            right = jnp.concatenate(
-                [blocks[f, q, pl.ds(2 * p, 2)].reshape(256, lt) for q in range(4)], axis=1)
-            product = lax.dot_general(left, right, NT, preferred_element_type=F32)
-            for half in range(2):
-                tile = product[:, half * 128:half * 128 + 128] * inv
-                for s in range(4):
-                    turned = [
-                        pltpu.roll(tile[s * 128 + r * 16:s * 128 + r * 16 + 16], (128 - 16 * r) % 128, 1)
-                        for r in range(8)
-                    ]
-                    for r in range(7):
-                        merged = jnp.where(lane < 112 - 16 * r, turned[r], turned[r + 1])
-                        stage[half, pl.ds(14 * per_class * s + 2 * r + f, 16, stride=14), :] = merged
-        for half in range(2):
-            place(2 * p + half, half)
-
-    base_index = len(pending)
-    assert base_index + 8 <= s_send.shape[0], base_index
-
-    def far(i, q):
-        m = 4 * i + 2
-        return pltpu.make_async_remote_copy(
-            src_ref=unit(q, m), dst_ref=unit(q, 18 + m), send_sem=s_send.at[base_index + 2 * i + q],
-            recv_sem=s_blk.at[q, 18 + m], device_id=d_sib, device_id_type=MESH)
-
-    def from_sibling(m):
-        for q in range(4):
-            got(q, 18 + m)
-
-    def early(i, _):
-        @pl.when(i == 4)
+
+        @pl.when((p == 8) & (core == 0))
         def _():
             for q in range(4):
-                got(q, 17, core == 0)
-
-        @pl.when((i > 5) | ((i == 5) & (core == 1)))
+                got(q, 17)
+
+        @pl.when(p > 8)
         def _():
-            from_sibling(4 * (i - 5))
-
-        @pl.when(i > 4)
-        def _():
-            from_sibling(4 * (i - 5) + 1)
+            for q in range(4):
+                got(q, 2 * p, (p > 9) | (core == 1))
+                got(q, 2 * p + 1)
 
         step(i)
-
-        @pl.when(i < 4)
-        def _():
-            for q in range(2):
-                got(q, 4 * i + 2)
-                far(i, q).start()
+        for at, runs in after.items():
+            @pl.when(i == at)
+            def _(runs=runs):
+                for run in runs:
+                    run()
         return 0
 
-    def late(i, _):
-        @pl.when(i > 12)
-        def _():
-            from_sibling(4 * (i - 13) + 2)
-            from_sibling(4 * (i - 13) + 3)
-
-        step(i)
-        return 0
-
-    lax.fori_loop(0, 9, early, 0)
-    for q in (2, 3):
-        y5(q, y2)
-    lax.fori_loop(9, 17, late, 0)
-    for i in range(4):
-        for q in range(2):
-            far(i, q).wait_send()
+    lax.fori_loop(0, 17, body, 0)
+    for f in range(2):
+        regroup(f)
+    put_tiles(pair_of(16))
+    for n in range(16):
+        pltpu.make_async_remote_copy(
+            src_ref=unit(0, 0), dst_ref=unit(0, 0), send_sem=s_send.at[base_index + n],
+            recv_sem=s_blk.at[0, 0], device_id=d_sib, device_id_type=MESH).wait_send()
     for cond, copy in pending:
         if cond is None:
             copy.wait_send()
@@ -490,6 +514,7 @@
             vm((4, 4, 2, sw, lt), BF16),
             vm((2, 4, 128, tokens), BF16),
             vm((2, 4, 37, 128, lt), BF16),
+            vm((2, 512, 256), F32),
             vm((2, 2 * tile_rows + 32, 128), F32),
             dma((320,)), dma((4,)), dma((4, 16)), dma((2, 4)), dma((4, 4)), dma((4, 4)), dma((4, 37)),
             dma(()),

time: 133 us -> 126 us (0.947); the launches traced: 131 us -> 126 us
  Pallas kernels: 128 us -> 123 us
    pallas_call x1, Pallas kernels: 128 us -> 123 us  [per_device(): pl.pallas_call(kernel, out_shape=vm((33, 2 * tile_rows, 128), BF16), in_s...]
where the time goes in v2:
time: 126 us
  Pallas kernels  123 us (98%)
  local copies, waits for them, and re-layouts  2.81 us (2%)
    pallas_call x1, Pallas kernels, per_device(): pl.pallas_call(kernel, out_shape=vm((33, 2 * tile_rows, 128), BF16), in_s...  123 us
    unnamed x1, local copies, waits for them, and re-layouts  2.81 us

profile of v2, /device:TPU:1, one launch (start us, length us, event | category | flops | bytes accessed | tf_op | source)
XLA Modules:
  0.0 126.2 jit_solution(9635338218867340748)
XLA Ops:
  0.0 123.4 %shard_map.46 = bf16[33,784,128]{2,1,0:T(8,128)(2,1)S(1)} custom-call(bf16[256,128]{1,0:T(8,128)(2,1)} %c_ref.1, bf16[448,2048]{1,0:T(8,128)(2,1)} %w_ref.1, bf16[448,256]{1,0:T(8,128)(2,1)} %bitcast.8, bf16[448,256]{1,0:T(8,128)(2,1)} %bitcast.9), custom_call_target="tpu_custom_call" | custom-call | tf_op jit(solution)/shard_map/pallas_call | solution.py:503
  123.4 2.8 %copy.7 = bf16[1,2,33,1,50176]{4,1,3,2,0:T(2,128)(2,1)} copy(bf16[1,2,33,1,50176]{4,1,3,2,0:T(2,128)(2,1)S(1)} %bitcast.7) | data formatting | bytes 13246464

commit v3 on v2

--- a/solution.py
+++ b/solution.py
@@ -55,6 +55,13 @@
         else:
             pl.when(cond)(copy.start)
         pending.append((cond, copy))
+
+    def drain(sends):
+        for cond, copy in sends:
+            if cond is None:
+                copy.wait_send()
+            else:
+                pl.when(cond)(copy.wait_send)
 
     def arrived(ref, sem, cond=None):
         wait = pltpu.make_async_copy(ref, ref, sem).wait
@@ -371,13 +378,15 @@
     b4(4)(1)
     rows_on(1)
     b4(12)(0)
+    rows_on(2)
     y4(y2)(2)
     b4(12)(1)
-    rows_on(2)
     y4(y2)(3)
     b4(8)(0)
     b4(8)(1)
     rows_on(3)
+    sent = len(pending) - 40
+    drain(pending[:sent])
     for q in range(4):
         rows_end(q)
 
@@ -427,10 +436,10 @@
             y_ref[k] = stage[half, 0:y_ref.shape[1], :].astype(BF16)
 
     def step(i):
+        put_tiles(pair_of(i - 2))
         for f in range(2):
             regroup(f)
             product(pair_of(i), f)
-        put_tiles(pair_of(i - 1))
 
     base_index = len(pending)
     assert base_index + 16 <= s_send.shape[0], base_index
@@ -479,6 +488,7 @@
         return 0
 
     lax.fori_loop(0, 17, body, 0)
+    put_tiles(pair_of(15))
     for f in range(2):
         regroup(f)
     put_tiles(pair_of(16))
@@ -486,11 +496,7 @@
         pltpu.make_async_remote_copy(
             src_ref=unit(0, 0), dst_ref=unit(0, 0), send_sem=s_send.at[base_index + n],
             recv_sem=s_blk.at[0, 0], device_id=d_sib, device_id_type=MESH).wait_send()
-    for cond, copy in pending:
-        if cond is None:
-            copy.wait_send()
-        else:
-            pl.when(cond)(copy.wait_send)
+    drain(pending[sent:])
 
 
 def per_device(cotangent, down_weight, gate_pre, up_pre):

time: 126 us -> 125 us (level)
  no operation moved by 1% of the time
where the time goes in v3:
time: 125 us
  Pallas kernels  122 us (98%)
  local copies, waits for them, and re-layouts  2.81 us (2%)
    pallas_call x1, Pallas kernels, per_device(): pl.pallas_call(kernel, out_shape=vm((33, 2 * tile_rows, 128), BF16), in_s...  122 us
    unnamed x1, local copies, waits for them, and re-layouts  2.81 us

profile of v3, /device:TPU:1, one launch (start us, length us, event | category | flops | bytes accessed | tf_op | source)
XLA Modules:
  0.0 125.3 jit_solution(2369828051090810448)
XLA Ops:
  0.0 122.4 %shard_map.46 = bf16[33,784,128]{2,1,0:T(8,128)(2,1)S(1)} custom-call(bf16[256,128]{1,0:T(8,128)(2,1)} %c_ref.1, bf16[448,2048]{1,0:T(8,128)(2,1)} %w_ref.1, bf16[448,256]{1,0:T(8,128)(2,1)} %bitcast.8, bf16[448,256]{1,0:T(8,128)(2,1)} %bitcast.9), custom_call_target="tpu_custom_call" | custom-call | tf_op jit(solution)/shard_map/pallas_call | solution.py:509
  122.5 2.8 %copy.7 = bf16[1,2,33,1,50176]{4,1,3,2,0:T(2,128)(2,1)} copy(bf16[1,2,33,1,50176]{4,1,3,2,0:T(2,128)(2,1)S(1)} %bitcast.7) | data formatting | bytes 13246464
